TPU v7x, 256 devices: a whole 4x4x8 slice. The times are simulated.
256 devices in a mesh: dp: 32 (over y, z_hi, core), centre: 8 (over x, z_lo).
Axes of the slice: x: 4, y: 4, z: 8 (z_hi: 4, z_lo: 2; z = z_hi * 2 + z_lo), core: 2. Of those that a mesh axis runs over, the one named last changes fastest.
Arguments:
- samples: float32 [16384, 512], P('dp'), may hold values from -4 to 4
- targets: float32 [16384, 64], P('dp'), may hold values from -6 to 6
- centres: float32 [32768, 512], P('centre'), may hold values from -4 to 4
- coefficients: float32 [32768, 64], P('centre'), may hold values from -0.9 to 0.9
Outputs:
- residual: float32 [16384, 64], P('dp')
- new_coefficients: float32 [32768, 64], P(('centre', 'dp'))
All inputs are finite; a program needn't handle non-finite values.
Results may differ from a plain program's by a relative error of at most 0.0001.
Values sent between devices are 32-bit elements; how exact they have to be, the bound alone decides.
A program may use at most 128 MiB of HBM per device.

v0:
```python
import functools
import math

import jax
import jax.numpy as jnp
from jax import lax
from jax.experimental import pallas as pl
from jax.experimental.pallas import tpu as pltpu
from jax.sharding import PartitionSpec as P

MESH = pl.DeviceIdType.MESH
f32, bf16 = jnp.float32, jnp.bfloat16
NT = (((1,), (1,)), ((), ()))

SOFTENING = 0.01
KERNEL_SCALE = 0.2
LEARNING_RATE = 4.0
SCALE_SQ = (math.log2(math.e) / KERNEL_SCALE) ** 2
EPS = SOFTENING * SCALE_SQ

PAIRS = ((0, 0), (0, 1), (1, 0), (3, 0), (1, 1), (3, 1), (2, 0), (2, 1))
PLACE = {pair: at for at, pair in enumerate(PAIRS)}
FIRST_ROWS = ((1, 0), (3, 0), (0, 1))
LATER_ROWS = ((2, 0), (2, 1), (1, 1), (3, 1))


def halves(x):
    hi = x.astype(bf16)
    lo = (x - hi.astype(f32)).astype(bf16)
    return hi, lo


def kernel_of(z):
    z = jnp.maximum(z, EPS)
    return jnp.exp2(-(z * lax.rsqrt(z)))


def lanes(x, times):
    return jnp.concatenate([x] * times, axis=1)


def step_kernel(
    samples, targets, centres, coefs, res_out, new_out,
    cen, cof, smp, tgt, rows,
    c3, ccol, crow, s3, scol, r3, rrow, cof2,
    kh, kl, th, tl,
    pacc, pred, pred_in, res, tgt_t, cof_t,
    gpart, g_y, gsum, g_z, gall,
    upart, u_core, usum, u_in, uall,
    vpart, v_core, vsum, v_in,
    lhs_r, lhs_u,
    loc_sem, smp_sem, row_send, row_recv, fwd_send, fwd_recv,
    p_send, p_recv, q_send, q_recv,
    gy_send, gy_recv, gz_send, gz_recv, az_send, az_recv, ay_send, ay_recv,
    uc_send, uc_recv, ur_send, ur_recv, bz_send, bz_recv, by_send, by_recv,
    vc_send, vc_recv, vr_send, vr_recv,
):
    d, c = lax.axis_index("dp"), lax.axis_index("centre")
    core, zh, y = d % 2, (d // 2) % 4, d // 8
    x, zl = c // 2, c % 2
    sib = d + 1 - 2 * core

    def at_y(j):
        return (((y + j) % 4 * 4 + zh) * 2 + core, c)

    def at_z(j):
        return ((y * 4 + (zh + j) % 4) * 2 + core, c)

    def centre_of(dx, dz):
        return (x + dx) % 4 * 2 + (zl + dz) % 2

    def remote(src, dst, send, recv, to):
        return pltpu.make_async_remote_copy(
            src_ref=src, dst_ref=dst, send_sem=send, recv_sem=recv, device_id=to, device_id_type=MESH
        )

    n = 128
    local = []

    def load(src, dst, sem):
        copy = pltpu.make_async_copy(src, dst, sem)
        copy.start()
        local.append(copy)
        return copy

    own_rows = pl.ds(pl.multiple_of(d * n, n), n)
    sib_rows = pl.ds(pl.multiple_of(sib * n, n), n)
    smp_load = load(samples, smp.at[0], loc_sem.at[0])
    cen_loads = []
    for b in range(16):
        owner = ((y + b // 4) % 4 * 4 + (zh + b % 4) % 4) * 2 + core
        at = pl.ds(pl.multiple_of(owner * n, n), n)
        cen_loads.append(load(centres.at[at], cen.at[pl.ds(b * n, n)], loc_sem.at[5 + b]))
    cof_loads = []
    for b in range(16):
        owner = ((y + b // 4) % 4 * 4 + (zh + b % 4) % 4) * 2 + core
        at = pl.ds(pl.multiple_of(owner * n, n), n)
        cof_loads.append(load(coefs.at[at], cof.at[pl.ds(b * n, n)], loc_sem.at[21 + b]))
    tgt_load = load(targets, tgt, loc_sem.at[1])
    row_loads = [
        load(centres.at[own_rows], rows.at[0, 0], loc_sem.at[2]),
        load(centres.at[sib_rows], rows.at[0, 1], loc_sem.at[3]),
    ]

    barrier = pltpu.get_barrier_semaphore()
    partners = [(sib, c)] + [at_y(j) for j in (1, 2, 3)] + [at_z(j) for j in (1, 2, 3)]
    for dx, dz in PAIRS[1:]:
        partners += [(d, centre_of(dx, dz)), (sib, centre_of(dx, dz))]
    for to in partners:
        pl.semaphore_signal(barrier, inc=1, device_id=to, device_id_type=MESH)
    pl.semaphore_wait(barrier, len(partners))

    sends = []
    smp_copy = remote(samples, smp.at[1], smp_sem.at[0], smp_sem.at[1], (sib, c))
    smp_copy.start()

    def send_rows(pairs):
        for dx, dz in pairs:
            j = PLACE[((4 - dx) % 4, dz)]
            copy = remote(
                centres.at[own_rows], rows.at[j, 0], row_send.at[PLACE[(dx, dz)]], row_recv.at[j], (d, centre_of(dx, dz))
            )
            copy.start()
            sends.append(copy)

    def forward_rows(j):
        remote(rows.at[j, 0], rows.at[j, 0], row_send.at[j], row_recv.at[j], (sib, c)).wait_recv()
        copy = remote(rows.at[j, 0], rows.at[j, 1], fwd_send.at[j], fwd_recv.at[j], (sib, c))
        copy.start()
        sends.append(copy)

    def await_forward(j):
        remote(rows.at[j, 0], rows.at[j, 1], fwd_send.at[j], fwd_recv.at[j], (sib, c)).wait_recv()

    send_rows(FIRST_ROWS)

    def norm_of(v):
        total = jnp.sum(v * v, axis=1, keepdims=True) * SCALE_SQ
        return jnp.broadcast_to(total, (n, n))

    def prepare_samples(half):
        def one(i, _):
            at = pl.ds(pl.multiple_of(i * n, n), n)
            to = pl.ds(pl.multiple_of(half * 512 + i * n, n), n)
            v = smp[half, at, :]
            hi, lo = halves(v * (-2.0 * SCALE_SQ))
            s3[to, 0:512] = hi
            s3[to, 512:1024] = hi
            s3[to, 1024:1536] = lo
            scol[to, :] = norm_of(v) + EPS
            return 0

        lax.fori_loop(0, 4, one, 0)

    def prepare_centres(i, _):
        at = pl.ds(pl.multiple_of(i * n, n), n)
        v = cen[at, :]
        hi, lo = halves(v)
        c3[at, 0:512] = hi
        c3[at, 512:1024] = lo
        c3[at, 1024:1536] = hi
        norms = norm_of(v)
        ccol[at, :] = norms + EPS
        crow[:, at] = norms.T[0:8, :]
        w = cof[at, :]
        whi = w.astype(bf16).astype(f32)
        cof2[at, :] = jnp.concatenate([whi, w - whi], axis=1).astype(bf16)
        return 0

    smp_load.wait()
    prepare_samples(0)
    for copy in cen_loads + cof_loads:
        copy.wait()
    lax.fori_loop(0, 16, prepare_centres, 0)
    smp_copy.wait_recv()
    prepare_samples(1)

    tn = 512
    pacc[...] = jnp.zeros_like(pacc)

    def data_tile(i, _):
        at = pl.ds(pl.multiple_of(i * tn, tn), tn)
        cross = lax.dot_general(s3[...], c3[at, :], NT, preferred_element_type=f32)
        value = kernel_of(cross + lanes(scol[...], tn // n) + crow[0:1, at])
        hi, lo = halves(value)
        kh[:, at] = hi
        kl[:, at] = lo
        w = cof2[at, :]
        pacc[...] += jnp.dot(hi, w, preferred_element_type=f32) + jnp.dot(lo, w, preferred_element_type=f32)
        return 0

    lax.fori_loop(0, 2048 // tn, data_tile, 0)
    both = pacc[...].T
    pred[...] = both[0:64] + both[64:128]

    group = [(dx, dz, kk) for dx, dz in PAIRS for kk in (0, 1)][1:]
    p_copies = []
    for s, (dx, dz, kk) in enumerate(group):
        to = centre_of(dx, dz)
        copy = remote(
            pred.at[pl.ds(pl.multiple_of(to * 8, 8), 8), pl.ds(kk * 512, 512)],
            pred_in.at[s], p_send.at[s], p_recv.at[s], (sib if kk else d, to),
        )
        copy.start()
        p_copies.append(copy)
    sends += p_copies

    tgt_load.wait()
    for copy in row_loads:
        copy.wait()
    wide = jnp.concatenate([tgt[...], jnp.zeros((512, 64), f32)], axis=1)
    tgt_t[...] = wide.T[0:64, :]
    wide = jnp.concatenate([cof[0:n, :], jnp.zeros((n, 64), f32)], axis=1)
    cof_t[...] = wide.T[0:64, :]

    tm = 512

    def square(j, _):
        for kk in (0, 1):
            v = rows[j, kk]
            hi, lo = halves(v * (-2.0 * SCALE_SQ))
            to = slice(kk * n, kk * n + n)
            r3[to, 0:512] = hi
            r3[to, 512:1024] = hi
            r3[to, 1024:1536] = lo
            rrow[:, to] = norm_of(v).T[0:8, :]
        cols = pl.ds(pl.multiple_of(j * 256, 256), 256)

        def tile(i, _):
            at = pl.ds(pl.multiple_of(i * tm, tm), tm)
            cross = lax.dot_general(c3[at, :], r3[...], NT, preferred_element_type=f32)
            hi, lo = halves(kernel_of(cross + lanes(ccol[at, :], 2) + rrow[0:1, :]))
            th[at, cols] = hi
            tl[at, cols] = lo
            return 0

        lax.fori_loop(0, 2048 // tm, tile, 0)
        return 0

    for pair in FIRST_ROWS:
        forward_rows(PLACE[pair])
    await_forward(PLACE[(0, 1)])
    lax.fori_loop(0, 2, square, 0)

    mine = pl.ds(pl.multiple_of(c * 8, 8), 8)
    for copy in p_copies:
        copy.wait_recv()
    total = pred[mine, 0:512] - tgt_t[mine, :]
    for s in range(15):
        total += pred_in[s]
    res[0, mine, :] = total
    q_copies = []
    for s, (dx, dz, kk) in enumerate(group):
        copy = remote(
            res.at[0, mine], res.at[kk, mine], q_send.at[s], q_recv.at[s], (sib if kk else d, centre_of(dx, dz))
        )
        copy.start()
        q_copies.append(copy)
    sends += q_copies
    await_forward(PLACE[(1, 0)])
    await_forward(PLACE[(3, 0)])
    lax.fori_loop(2, 4, square, 0)
    for copy in q_copies:
        copy.wait_recv()
    send_rows(LATER_ROWS)

    for kk in (0, 1):
        hi, lo = halves(res[kk])
        lhs_r[0:64, kk * 512 : kk * 512 + 512] = lo
        lhs_r[64:128, kk * 512 : kk * 512 + 512] = hi
    gy_copies = []
    for dy in (2, 1, 3, 0):
        at = slice(dy * 512, dy * 512 + 512)
        a = jnp.dot(lhs_r[...], kh[:, at], preferred_element_type=f32)
        b = jnp.dot(lhs_r[64:128, :], kl[:, at], preferred_element_type=f32)
        gpart[dy] = a[0:64] + a[64:128] + b
        if dy:
            copy = remote(gpart.at[dy], g_y.at[dy - 1], gy_send.at[dy - 1], gy_recv.at[dy - 1], at_y(dy))
            copy.start()
            gy_copies.append(copy)
    sends += gy_copies
    res_out[...] = res[0]
    for pair in LATER_ROWS:
        forward_rows(PLACE[pair])
    await_forward(4)
    lax.fori_loop(4, 5, square, 0)
    for copy in gy_copies:
        copy.wait_recv()
    gsum[...] = gpart[0] + g_y[0] + g_y[1] + g_y[2]
    gz_copies = []
    for dz in (2, 1, 3):
        copy = remote(
            gsum.at[:, pl.ds(dz * n, n)], g_z.at[dz - 1], gz_send.at[dz - 1], gz_recv.at[dz - 1], at_z(dz)
        )
        copy.start()
        gz_copies.append(copy)
    sends += gz_copies
    await_forward(5)
    lax.fori_loop(5, 6, square, 0)
    for copy in gz_copies:
        copy.wait_recv()
    gall[0, :, 0:n] = gsum[:, 0:n] + g_z[0] + g_z[1] + g_z[2]

    def spread_z(buf, send, recv):
        copies = []
        for dz in (2, 1, 3):
            to = (4 - dz) % 4
            copy = remote(
                buf.at[0, :, pl.ds(0, n)], buf.at[0, :, pl.ds(to * n, n)], send.at[dz - 1], recv.at[dz - 1], at_z(dz)
            )
            copy.start()
            copies.append(copy)
        sends.extend(copies)
        return copies

    def spread_y(buf, send, recv):
        copies = []
        for dy in (2, 1, 3):
            copy = remote(buf.at[0], buf.at[(4 - dy) % 4], send.at[dy - 1], recv.at[dy - 1], at_y(dy))
            copy.start()
            copies.append(copy)
        sends.extend(copies)
        return copies

    az_copies = spread_z(gall, az_send, az_recv)
    await_forward(6)
    lax.fori_loop(6, 7, square, 0)
    for copy in az_copies:
        copy.wait_recv()
    ay_copies = spread_y(gall, ay_send, ay_recv)
    await_forward(7)
    lax.fori_loop(7, 8, square, 0)
    for copy in ay_copies:
        copy.wait_recv()

    def project(buf, out, ones):
        for dy in range(4):
            hi, lo = halves(buf[dy, 0:64, :])
            lhs_u[0:64, dy * 512 : dy * 512 + 512] = lo
            lhs_u[64:128, dy * 512 : dy * 512 + 512] = hi
        if ones:
            lhs_u[128:144, :] = jnp.ones((16, 2048), bf16)
        top = 144 if ones else 128

        def tile(i, _):
            at = pl.ds(pl.multiple_of(i * 512, 512), 512)
            a = jnp.dot(lhs_u[0:top, :], th[:, at], preferred_element_type=f32)
            b = jnp.dot(lhs_u[64:top, :], tl[:, at], preferred_element_type=f32)
            out[0:64, at] = a[0:64] + a[64:128] + b[0:64]
            if ones:
                out[64:72, at] = a[128:136] + b[64:72]
            return 0

        lax.fori_loop(0, 4, tile, 0)

    def swap_core(part, arrived, send, recv):
        copies = []
        for j in range(8):
            copy = remote(part.at[:, pl.ds((2 * j + 1) * n, n)], arrived.at[j], send.at[j], recv.at[j], (sib, c))
            copy.start()
            copies.append(copy)
        sends.extend(copies)
        for copy in copies:
            copy.wait_recv()

    def to_owners(summed, arrived, send, recv):
        copies = []
        for j, (dx, dz) in enumerate(PAIRS):
            if j:
                copy = remote(
                    summed.at[j], arrived.at[j - 1], send.at[j - 1], recv.at[j - 1], (d, centre_of(dx, dz))
                )
                copy.start()
                copies.append(copy)
        sends.extend(copies)
        for copy in copies:
            copy.wait_recv()

    project(gall, upart, True)
    swap_core(upart, u_core, uc_send, uc_recv)
    for j in range(8):
        usum[j] = upart[:, 2 * j * n : 2 * j * n + n] + u_core[j]
    to_owners(usum, u_in, ur_send, ur_recv)
    total = usum[0]
    for s in range(7):
        total += u_in[s]
    uall[0, 0:64, 0:n] = total[0:64]
    uall[0, 64:72, 0:n] = jnp.broadcast_to(jnp.max(total[64:72], axis=1, keepdims=True), (8, n))

    for copy in spread_z(uall, bz_send, bz_recv):
        copy.wait_recv()
    for copy in spread_y(uall, by_send, by_recv):
        copy.wait_recv()

    project(uall, vpart, False)
    largest = uall[0, 64:72, 0:n]
    for dy in range(4):
        for dz in range(4):
            largest = jnp.maximum(largest, uall[dy, 64:72, dz * n : dz * n + n])
    for j in range(16):
        vpart[64:72, j * n : j * n + n] = largest
    swap_core(vpart, v_core, vc_send, vc_recv)
    for j in range(8):
        vsum[j, 0:64] = vpart[0:64, 2 * j * n : 2 * j * n + n] + v_core[j, 0:64]
        vsum[j, 64:72] = jnp.maximum(largest, v_core[j, 64:72])
    to_owners(vsum, v_in, vr_send, vr_recv)
    twice = vsum[0, 0:64]
    largest = vsum[0, 64:72]
    for s in range(7):
        twice += v_in[s, 0:64]
        largest = jnp.maximum(largest, v_in[s, 64:72])
    size = jnp.concatenate([1.0 / largest] * 8, axis=0)
    once, grad = uall[0, 0:64, 0:n], gall[0, :, 0:n]
    theta = size * (3.0 * grad - size * (3.0 * once - size * twice))
    new_out[...] = cof_t[...] - LEARNING_RATE * theta

    smp_copy.wait_send()
    for copy in sends:
        copy.wait_send()


def body(samples, targets, centres, coefficients):
    dma = pltpu.SemaphoreType.DMA
    vmem = pltpu.VMEM
    res_t, new_t = pl.pallas_call(
        step_kernel,
        out_shape=(jax.ShapeDtypeStruct((64, 512), f32), jax.ShapeDtypeStruct((64, 128), f32)),
        in_specs=[pl.BlockSpec(memory_space=pl.ANY)] * 4,
        out_specs=[pl.BlockSpec(memory_space=vmem)] * 2,
        scratch_shapes=[
            vmem((2048, 512), f32), vmem((2048, 64), f32), vmem((2, 512, 512), f32), vmem((512, 64), f32),
            vmem((8, 2, 128, 512), f32),
            vmem((2048, 1536), bf16), vmem((2048, 128), f32), vmem((8, 2048), f32),
            vmem((1024, 1536), bf16), vmem((1024, 128), f32), vmem((256, 1536), bf16), vmem((8, 256), f32),
            vmem((2048, 128), bf16),
            vmem((1024, 2048), bf16), vmem((1024, 2048), bf16), vmem((2048, 2048), bf16), vmem((2048, 2048), bf16),
            vmem((1024, 128), f32), vmem((64, 1024), f32), vmem((15, 8, 512), f32), vmem((2, 64, 512), f32),
            vmem((64, 512), f32), vmem((64, 128), f32),
            vmem((4, 64, 512), f32), vmem((3, 64, 512), f32), vmem((64, 512), f32), vmem((3, 64, 128), f32),
            vmem((4, 64, 512), f32),
            vmem((72, 2048), f32), vmem((8, 72, 128), f32), vmem((8, 72, 128), f32), vmem((7, 72, 128), f32),
            vmem((4, 72, 512), f32),
            vmem((72, 2048), f32), vmem((8, 72, 128), f32), vmem((8, 72, 128), f32), vmem((7, 72, 128), f32),
            vmem((128, 1024), bf16), vmem((144, 2048), bf16),
            dma((37,)), dma((2,)), dma((8,)), dma((8,)), dma((8,)), dma((8,)),
            dma((15,)), dma((15,)), dma((15,)), dma((15,)),
            dma((3,)), dma((3,)), dma((3,)), dma((3,)), dma((3,)), dma((3,)), dma((3,)), dma((3,)),
            dma((8,)), dma((8,)), dma((7,)), dma((7,)), dma((3,)), dma((3,)), dma((3,)), dma((3,)),
            dma((8,)), dma((8,)), dma((7,)), dma((7,)),
        ],
        compiler_params=pltpu.CompilerParams(
            collective_id=0, has_side_effects=True, vmem_limit_bytes=63 * 2**20
        ),
    )(samples, targets, centres, coefficients)
    return res_t.T, new_t.T


def solution(mesh):
    return jax.shard_map(
        body,
        mesh=mesh,
        in_specs=(P("dp", None), P("dp", None), P("centre", None), P("centre", None)),
        out_specs=(P("dp", None), P(("centre", "dp"), None)),
        check_vma=False,
    )
```

profile of v0, /device:TPU:1, one launch (start us, length us, event | category | flops | bytes accessed | tf_op | source)
XLA Modules:
  0.0 130.1 jit_solution(9264157617590570850)
XLA Ops:
  0.6 1.8 %copy.6.targets = f32[512,64]{1,0:T(8,128)} copy(f32[512,64]{0,1:T(8,128)} %param.5) | data formatting | bytes 262144 | tf_op args[1]
  2.4 3.2 %copy.7.coefs = f32[4096,64]{1,0:T(8,128)} copy(f32[4096,64]{0,1:T(8,128)} %param.7) | data formatting | bytes 2097152 | tf_op args[3]
  5.6 121.6 %shard_map.59 = (f32[64,512]{1,0:T(8,128)}, f32[64,128]{1,0:T(8,128)}) custom-call(f32[512,512]{1,0:T(8,128)} %samples.1, f32[512,64]{1,0:T(8,128)} %copy.6.targets, f32[4096,512]{1,0:T(8,128)} %centres.1, f32[4096,64]{1,0:T(8,128)} %copy.7.coefs), custom_call_target="tpu_custom_call" | custom-call | tf_op jit(solution)/shard_map/pallas_call | solution.py:425
  127.2 1.6 %copy.10 = f32[512,64]{0,1:T(8,128)} copy(f32[512,64]{0,1:T(8,128)} %bitcast.2) | data formatting | bytes 262144
  128.7 1.4 %copy.11 = f32[128,64]{0,1:T(8,128)} copy(f32[128,64]{0,1:T(8,128)} %bitcast.3) | data formatting | bytes 65536
where the time goes:
time: 130 us
  Pallas kernels  122 us (94%)
  local copies, waits for them, and re-layouts  7.9 us (6%)
    pallas_call x1, Pallas kernels, body(): pl.pallas_call(step_kernel, out_shape=(jax.ShapeDtypeStruct((64, 512), f3...  122 us
    unnamed x4, local copies, waits for them, and re-layouts  7.9 us

commit v1 on v0

--- a/solution.py
+++ b/solution.py
@@ -18,10 +18,10 @@
 SCALE_SQ = (math.log2(math.e) / KERNEL_SCALE) ** 2
 EPS = SOFTENING * SCALE_SQ
 
-PAIRS = ((0, 0), (0, 1), (1, 0), (3, 0), (1, 1), (3, 1), (2, 0), (2, 1))
+PAIRS = ((0, 0), (0, 1), (1, 0), (3, 0), (2, 0), (1, 1), (3, 1), (2, 1))
 PLACE = {pair: at for at, pair in enumerate(PAIRS)}
 FIRST_ROWS = ((1, 0), (3, 0), (0, 1))
-LATER_ROWS = ((2, 0), (2, 1), (1, 1), (3, 1))
+LATER_ROWS = ((1, 1), (3, 1))
 
 
 def halves(x):
@@ -44,12 +44,12 @@
     cen, cof, smp, tgt, rows,
     c3, ccol, crow, s3, scol, r3, rrow, cof2,
     kh, kl, th, tl,
-    pacc, pred, pred_in, res, tgt_t, cof_t,
+    pacc, pred, pred_in, res,
     gpart, g_y, gsum, g_z, gall,
     upart, u_core, usum, u_in, uall,
     vpart, v_core, vsum, v_in,
     lhs_r, lhs_u,
-    loc_sem, smp_sem, row_send, row_recv, fwd_send, fwd_recv,
+    loc_sem, smp_send, smp_recv, row_send, row_recv, fwd_send, fwd_recv, rel_send, rel_recv,
     p_send, p_recv, q_send, q_recv,
     gy_send, gy_recv, gz_send, gz_recv, az_send, az_recv, ay_send, ay_recv,
     uc_send, uc_recv, ur_send, ur_recv, bz_send, bz_recv, by_send, by_recv,
@@ -95,7 +95,7 @@
     for b in range(16):
         owner = ((y + b // 4) % 4 * 4 + (zh + b % 4) % 4) * 2 + core
         at = pl.ds(pl.multiple_of(owner * n, n), n)
-        cof_loads.append(load(coefs.at[at], cof.at[pl.ds(b * n, n)], loc_sem.at[21 + b]))
+        cof_loads.append(load(coefs.at[:, at], cof.at[:, pl.ds(b * n, n)], loc_sem.at[21 + b]))
     tgt_load = load(targets, tgt, loc_sem.at[1])
     row_loads = [
         load(centres.at[own_rows], rows.at[0, 0], loc_sem.at[2]),
@@ -111,20 +111,45 @@
     pl.semaphore_wait(barrier, len(partners))
 
     sends = []
-    smp_copy = remote(samples, smp.at[1], smp_sem.at[0], smp_sem.at[1], (sib, c))
-    smp_copy.start()
+    smp_load.wait()
+    smp_copies = []
+    for i in range(4):
+        at = pl.ds(i * n, n)
+        copy = remote(smp.at[0, at], smp.at[1, at], smp_send.at[i], smp_recv.at[i], (sib, c))
+        copy.start()
+        smp_copies.append(copy)
+    sends += smp_copies
+    cen_loads[0].wait()
 
     def send_rows(pairs):
         for dx, dz in pairs:
             j = PLACE[((4 - dx) % 4, dz)]
             copy = remote(
-                centres.at[own_rows], rows.at[j, 0], row_send.at[PLACE[(dx, dz)]], row_recv.at[j], (d, centre_of(dx, dz))
+                cen.at[pl.ds(0, n)], rows.at[j, 0], row_send.at[PLACE[(dx, dz)]], row_recv.at[j], (d, centre_of(dx, dz))
             )
             copy.start()
             sends.append(copy)
 
+    def await_rows(j):
+        remote(rows.at[j, 0], rows.at[j, 0], row_send.at[j], row_recv.at[j], (sib, c)).wait_recv()
+
+    def relay_rows(dz):
+        far = PLACE[(2, dz)]
+        for i, (back, on) in enumerate(((1, 3), (3, 1))):
+            part = pl.ds(i * 64, 64)
+            copy = remote(
+                rows.at[PLACE[(back, dz)], 0, part], rows.at[far, 0, part],
+                rel_send.at[dz * 2 + i], rel_recv.at[dz * 2 + i], (d, centre_of(on, 0)),
+            )
+            copy.start()
+            sends.append(copy)
+
+    def await_relayed(dz):
+        for i in (0, 1):
+            part = rows.at[PLACE[(2, dz)], 0, pl.ds(i * 64, 64)]
+            remote(part, part, rel_send.at[dz * 2 + i], rel_recv.at[dz * 2 + i], (sib, c)).wait_recv()
+
     def forward_rows(j):
-        remote(rows.at[j, 0], rows.at[j, 0], row_send.at[j], row_recv.at[j], (sib, c)).wait_recv()
         copy = remote(rows.at[j, 0], rows.at[j, 1], fwd_send.at[j], fwd_recv.at[j], (sib, c))
         copy.start()
         sends.append(copy)
@@ -162,34 +187,42 @@
         norms = norm_of(v)
         ccol[at, :] = norms + EPS
         crow[:, at] = norms.T[0:8, :]
-        w = cof[at, :]
+        w = cof[:, at]
         whi = w.astype(bf16).astype(f32)
-        cof2[at, :] = jnp.concatenate([whi, w - whi], axis=1).astype(bf16)
+        cof2[at, :] = jnp.concatenate([whi, w - whi], axis=0).T.astype(bf16)
         return 0
 
-    smp_load.wait()
     prepare_samples(0)
-    for copy in cen_loads + cof_loads:
+    for copy in cen_loads[1:] + cof_loads:
         copy.wait()
     lax.fori_loop(0, 16, prepare_centres, 0)
-    smp_copy.wait_recv()
-    prepare_samples(1)
 
     tn = 512
     pacc[...] = jnp.zeros_like(pacc)
 
     def data_tile(i, _):
-        at = pl.ds(pl.multiple_of(i * tn, tn), tn)
-        cross = lax.dot_general(s3[...], c3[at, :], NT, preferred_element_type=f32)
-        value = kernel_of(cross + lanes(scol[...], tn // n) + crow[0:1, at])
+        mine = pl.ds(pl.multiple_of(i // 4 * 512, 512), 512)
+        at = pl.ds(pl.multiple_of(i % 4 * tn, tn), tn)
+        cross = lax.dot_general(s3[mine, :], c3[at, :], NT, preferred_element_type=f32)
+        value = kernel_of(cross + lanes(scol[mine, :], tn // n) + crow[0:1, at])
         hi, lo = halves(value)
-        kh[:, at] = hi
-        kl[:, at] = lo
+        kh[mine, at] = hi
+        kl[mine, at] = lo
         w = cof2[at, :]
-        pacc[...] += jnp.dot(hi, w, preferred_element_type=f32) + jnp.dot(lo, w, preferred_element_type=f32)
+        pacc[mine, :] += jnp.dot(hi, w, preferred_element_type=f32) + jnp.dot(lo, w, preferred_element_type=f32)
         return 0
 
-    lax.fori_loop(0, 2048 // tn, data_tile, 0)
+    lax.fori_loop(0, 4, data_tile, 0)
+    for copy in smp_copies:
+        copy.wait_recv()
+    prepare_samples(1)
+    lax.fori_loop(4, 6, data_tile, 0)
+    for pair in FIRST_ROWS:
+        await_rows(PLACE[pair])
+    relay_rows(0)
+    for pair in FIRST_ROWS[::-1]:
+        forward_rows(PLACE[pair])
+    lax.fori_loop(6, 8, data_tile, 0)
     both = pacc[...].T
     pred[...] = both[0:64] + both[64:128]
 
@@ -208,10 +241,6 @@
     tgt_load.wait()
     for copy in row_loads:
         copy.wait()
-    wide = jnp.concatenate([tgt[...], jnp.zeros((512, 64), f32)], axis=1)
-    tgt_t[...] = wide.T[0:64, :]
-    wide = jnp.concatenate([cof[0:n, :], jnp.zeros((n, 64), f32)], axis=1)
-    cof_t[...] = wide.T[0:64, :]
 
     tm = 512
 
@@ -237,15 +266,12 @@
         lax.fori_loop(0, 2048 // tm, tile, 0)
         return 0
 
-    for pair in FIRST_ROWS:
-        forward_rows(PLACE[pair])
-    await_forward(PLACE[(0, 1)])
-    lax.fori_loop(0, 2, square, 0)
+    lax.fori_loop(0, 1, square, 0)
 
     mine = pl.ds(pl.multiple_of(c * 8, 8), 8)
     for copy in p_copies:
         copy.wait_recv()
-    total = pred[mine, 0:512] - tgt_t[mine, :]
+    total = pred[mine, 0:512] - tgt[mine, :]
     for s in range(15):
         total += pred_in[s]
     res[0, mine, :] = total
@@ -257,9 +283,11 @@
         copy.start()
         q_copies.append(copy)
     sends += q_copies
-    await_forward(PLACE[(1, 0)])
-    await_forward(PLACE[(3, 0)])
-    lax.fori_loop(2, 4, square, 0)
+    await_relayed(0)
+    forward_rows(PLACE[(2, 0)])
+    await_forward(1)
+    await_forward(2)
+    lax.fori_loop(1, 3, square, 0)
     for copy in q_copies:
         copy.wait_recv()
     send_rows(LATER_ROWS)
@@ -280,10 +308,9 @@
             gy_copies.append(copy)
     sends += gy_copies
     res_out[...] = res[0]
-    for pair in LATER_ROWS:
-        forward_rows(PLACE[pair])
+    await_forward(3)
     await_forward(4)
-    lax.fori_loop(4, 5, square, 0)
+    lax.fori_loop(3, 5, square, 0)
     for copy in gy_copies:
         copy.wait_recv()
     gsum[...] = gpart[0] + g_y[0] + g_y[1] + g_y[2]
@@ -295,8 +322,11 @@
         copy.start()
         gz_copies.append(copy)
     sends += gz_copies
-    await_forward(5)
-    lax.fori_loop(5, 6, square, 0)
+    for pair in LATER_ROWS:
+        await_rows(PLACE[pair])
+    relay_rows(1)
+    for pair in LATER_ROWS:
+        forward_rows(PLACE[pair])
     for copy in gz_copies:
         copy.wait_recv()
     gall[0, :, 0:n] = gsum[:, 0:n] + g_z[0] + g_z[1] + g_z[2]
@@ -323,64 +353,75 @@
         return copies
 
     az_copies = spread_z(gall, az_send, az_recv)
+    await_forward(5)
     await_forward(6)
-    lax.fori_loop(6, 7, square, 0)
+    lax.fori_loop(5, 7, square, 0)
     for copy in az_copies:
         copy.wait_recv()
+    await_relayed(1)
+    forward_rows(7)
     ay_copies = spread_y(gall, ay_send, ay_recv)
     await_forward(7)
     lax.fori_loop(7, 8, square, 0)
-    for copy in ay_copies:
-        copy.wait_recv()
-
-    def project(buf, out, ones):
-        for dy in range(4):
+    def project(buf, out, arrivals, ones, finish):
+        top = 144 if ones else 128
+        for dy in (0, 1, 3, 2):
+            if dy:
+                arrivals[(4 - dy) % 4].wait_recv()
             hi, lo = halves(buf[dy, 0:64, :])
-            lhs_u[0:64, dy * 512 : dy * 512 + 512] = lo
-            lhs_u[64:128, dy * 512 : dy * 512 + 512] = hi
-        if ones:
-            lhs_u[128:144, :] = jnp.ones((16, 2048), bf16)
-        top = 144 if ones else 128
-
-        def tile(i, _):
-            at = pl.ds(pl.multiple_of(i * 512, 512), 512)
-            a = jnp.dot(lhs_u[0:top, :], th[:, at], preferred_element_type=f32)
-            b = jnp.dot(lhs_u[64:top, :], tl[:, at], preferred_element_type=f32)
-            out[0:64, at] = a[0:64] + a[64:128] + b[0:64]
-            if ones:
-                out[64:72, at] = a[128:136] + b[64:72]
-            return 0
-
-        lax.fori_loop(0, 4, tile, 0)
-
-    def swap_core(part, arrived, send, recv):
-        copies = []
-        for j in range(8):
-            copy = remote(part.at[:, pl.ds((2 * j + 1) * n, n)], arrived.at[j], send.at[j], recv.at[j], (sib, c))
-            copy.start()
-            copies.append(copy)
-        sends.extend(copies)
-        for copy in copies:
-            copy.wait_recv()
-
-    def to_owners(summed, arrived, send, recv):
-        copies = []
-        for j, (dx, dz) in enumerate(PAIRS):
-            if j:
-                copy = remote(
-                    summed.at[j], arrived.at[j - 1], send.at[j - 1], recv.at[j - 1], (d, centre_of(dx, dz))
-                )
-                copy.start()
-                copies.append(copy)
-        sends.extend(copies)
-        for copy in copies:
-            copy.wait_recv()
-
-    project(gall, upart, True)
-    swap_core(upart, u_core, uc_send, uc_recv)
-    for j in range(8):
+            lhs_u[0:64, :] = lo
+            lhs_u[64:128, :] = hi
+            k = slice(dy * 512, dy * 512 + 512)
+
+            def part(at):
+                a = jnp.dot(lhs_u[0:top, :], th[k, at], preferred_element_type=f32)
+                b = jnp.dot(lhs_u[64:top, :], tl[k, at], preferred_element_type=f32)
+                total = a[0:64] + a[64:128] + b[0:64]
+                out[0:64, at] = total if dy == 0 else out[0:64, at] + total
+                if ones:
+                    total = a[128:136] + b[64:72]
+                    out[64:72, at] = total if dy == 0 else out[64:72, at] + total
+
+            if dy == 2:
+                for i in (3, 2, 1, 0):
+                    part(slice(i * 512, i * 512 + 512))
+                    finish(2 * i + 1)
+                    finish(2 * i)
+            else:
+
+                def tile(i, _):
+                    part(pl.ds(pl.multiple_of(i * 512, 512), 512))
+                    return 0
+
+                lax.fori_loop(0, 4, tile, 0)
+
+    def swap_core(part, arrived, send, recv, j):
+        copy = remote(part.at[:, pl.ds((2 * j + 1) * n, n)], arrived.at[j], send.at[j], recv.at[j], (sib, c))
+        copy.start()
+        sends.append(copy)
+        return copy
+
+    def to_owner(summed, arrived, send, recv, j):
+        copy = remote(summed.at[j], arrived.at[j - 1], send.at[j - 1], recv.at[j - 1], (d, centre_of(*PAIRS[j])))
+        copy.start()
+        sends.append(copy)
+        return copy
+
+    lhs_u[128:144, :] = jnp.ones((16, 512), bf16)
+    swaps = {}
+
+    def finish_u(j):
+        swaps[j] = swap_core(upart, u_core, uc_send, uc_recv, j)
+
+    project(gall, upart, {i: copy for i, copy in zip((2, 1, 3), ay_copies)}, True, finish_u)
+    owners = []
+    for j in (7, 6, 5, 4, 3, 2, 1, 0):
+        swaps[j].wait_recv()
         usum[j] = upart[:, 2 * j * n : 2 * j * n + n] + u_core[j]
-    to_owners(usum, u_in, ur_send, ur_recv)
+        if j:
+            owners.append(to_owner(usum, u_in, ur_send, ur_recv, j))
+    for copy in owners:
+        copy.wait_recv()
     total = usum[0]
     for s in range(7):
         total += u_in[s]
@@ -389,21 +430,30 @@
 
     for copy in spread_z(uall, bz_send, bz_recv):
         copy.wait_recv()
-    for copy in spread_y(uall, by_send, by_recv):
-        copy.wait_recv()
-
-    project(uall, vpart, False)
-    largest = uall[0, 64:72, 0:n]
-    for dy in range(4):
-        for dz in range(4):
-            largest = jnp.maximum(largest, uall[dy, 64:72, dz * n : dz * n + n])
-    for j in range(16):
-        vpart[64:72, j * n : j * n + n] = largest
-    swap_core(vpart, v_core, vc_send, vc_recv)
-    for j in range(8):
+    by_copies = spread_y(uall, by_send, by_recv)
+
+    tops = []
+
+    def finish_v(j):
+        if not tops:
+            largest = uall[0, 64:72, 0:n]
+            for dy in range(4):
+                for dz in range(4):
+                    largest = jnp.maximum(largest, uall[dy, 64:72, dz * n : dz * n + n])
+            tops.append(largest)
+        vpart[64:72, (2 * j + 1) * n : (2 * j + 2) * n] = tops[0]
+        swaps[j] = swap_core(vpart, v_core, vc_send, vc_recv, j)
+
+    project(uall, vpart, {i: copy for i, copy in zip((2, 1, 3), by_copies)}, False, finish_v)
+    owners = []
+    for j in (7, 6, 5, 4, 3, 2, 1, 0):
+        swaps[j].wait_recv()
         vsum[j, 0:64] = vpart[0:64, 2 * j * n : 2 * j * n + n] + v_core[j, 0:64]
-        vsum[j, 64:72] = jnp.maximum(largest, v_core[j, 64:72])
-    to_owners(vsum, v_in, vr_send, vr_recv)
+        vsum[j, 64:72] = jnp.maximum(tops[0], v_core[j, 64:72])
+        if j:
+            owners.append(to_owner(vsum, v_in, vr_send, vr_recv, j))
+    for copy in owners:
+        copy.wait_recv()
     twice = vsum[0, 0:64]
     largest = vsum[0, 64:72]
     for s in range(7):
@@ -412,11 +462,15 @@
     size = jnp.concatenate([1.0 / largest] * 8, axis=0)
     once, grad = uall[0, 0:64, 0:n], gall[0, :, 0:n]
     theta = size * (3.0 * grad - size * (3.0 * once - size * twice))
-    new_out[...] = cof_t[...] - LEARNING_RATE * theta
-
-    smp_copy.wait_send()
+    new_out[...] = cof[:, 0:n] - LEARNING_RATE * theta
+
     for copy in sends:
         copy.wait_send()
+
+
+def hand_over(res_in, new_in, res_out, new_out):
+    res_out[...] = res_in[...]
+    new_out[...] = new_in[...]
 
 
 def body(samples, targets, centres, coefficients):
@@ -428,21 +482,20 @@
         in_specs=[pl.BlockSpec(memory_space=pl.ANY)] * 4,
         out_specs=[pl.BlockSpec(memory_space=vmem)] * 2,
         scratch_shapes=[
-            vmem((2048, 512), f32), vmem((2048, 64), f32), vmem((2, 512, 512), f32), vmem((512, 64), f32),
+            vmem((2048, 512), f32), vmem((64, 2048), f32), vmem((2, 512, 512), f32), vmem((64, 512), f32),
             vmem((8, 2, 128, 512), f32),
             vmem((2048, 1536), bf16), vmem((2048, 128), f32), vmem((8, 2048), f32),
             vmem((1024, 1536), bf16), vmem((1024, 128), f32), vmem((256, 1536), bf16), vmem((8, 256), f32),
             vmem((2048, 128), bf16),
             vmem((1024, 2048), bf16), vmem((1024, 2048), bf16), vmem((2048, 2048), bf16), vmem((2048, 2048), bf16),
             vmem((1024, 128), f32), vmem((64, 1024), f32), vmem((15, 8, 512), f32), vmem((2, 64, 512), f32),
-            vmem((64, 512), f32), vmem((64, 128), f32),
             vmem((4, 64, 512), f32), vmem((3, 64, 512), f32), vmem((64, 512), f32), vmem((3, 64, 128), f32),
             vmem((4, 64, 512), f32),
             vmem((72, 2048), f32), vmem((8, 72, 128), f32), vmem((8, 72, 128), f32), vmem((7, 72, 128), f32),
             vmem((4, 72, 512), f32),
             vmem((72, 2048), f32), vmem((8, 72, 128), f32), vmem((8, 72, 128), f32), vmem((7, 72, 128), f32),
-            vmem((128, 1024), bf16), vmem((144, 2048), bf16),
-            dma((37,)), dma((2,)), dma((8,)), dma((8,)), dma((8,)), dma((8,)),
+            vmem((128, 1024), bf16), vmem((144, 512), bf16),
+            dma((37,)), dma((4,)), dma((4,)), dma((8,)), dma((8,)), dma((8,)), dma((8,)), dma((4,)), dma((4,)),
             dma((15,)), dma((15,)), dma((15,)), dma((15,)),
             dma((3,)), dma((3,)), dma((3,)), dma((3,)), dma((3,)), dma((3,)), dma((3,)), dma((3,)),
             dma((8,)), dma((8,)), dma((7,)), dma((7,)), dma((3,)), dma((3,)), dma((3,)), dma((3,)),
@@ -451,7 +504,13 @@
         compiler_params=pltpu.CompilerParams(
             collective_id=0, has_side_effects=True, vmem_limit_bytes=63 * 2**20
         ),
-    )(samples, targets, centres, coefficients)
+    )(samples, targets.T, centres, coefficients.T)
+    res_t, new_t = pl.pallas_call(
+        hand_over,
+        out_shape=(jax.ShapeDtypeStruct((64, 512), f32), jax.ShapeDtypeStruct((64, 128), f32)),
+        in_specs=[pl.BlockSpec(memory_space=vmem)] * 2,
+        out_specs=[pl.BlockSpec(memory_space=vmem)] * 2,
+    )(res_t, new_t)
     return res_t.T, new_t.T
 
 

time: 130 us -> 107 us (0.82)
  Pallas kernels: 122 us -> 107 us
  local copies, waits for them, and re-layouts: 7.9 us -> 0 us
    pallas_call x1, Pallas kernels: 122 us -> 105 us  [body(): pl.pallas_call(step_kernel, out_shape=(jax.ShapeDtypeStruct((64, 512), f3...]
    unnamed x4 -> x0, local copies, waits for them, and re-layouts: 7.9 us -> none
    pallas_call x0 -> x1, Pallas kernels: none -> 1.57 us  [body(): pl.pallas_call(hand_over, out_shape=(jax.ShapeDtypeStruct((64, 512), f32)...]
where the time goes in v1:
time: 107 us
  Pallas kernels  107 us (100%)
    pallas_call x1, Pallas kernels, body(): pl.pallas_call(step_kernel, out_shape=(jax.ShapeDtypeStruct((64, 512), f3...  105 us

profile of v1, /device:TPU:1, one launch (start us, length us, event | category | flops | bytes accessed | tf_op | source)
XLA Modules:
  0.0 107.3 jit_solution(2295122798962733544)
XLA Ops:
  0.6 105.0 %shard_map.59 = (f32[64,512]{1,0:T(8,128)}, f32[64,128]{1,0:T(8,128)}) custom-call(f32[512,512]{1,0:T(8,128)} %samples.1, f32[64,512]{1,0:T(8,128)} %bitcast.5, f32[4096,512]{1,0:T(8,128)} %centres.1, f32[64,4096]{1,0:T(8,128)} %bitcast.4), custom_call_target="tpu_custom_call" | custom-call | tf_op jit(solution)/shard_map/pallas_call | solution.py:479
  105.7 1.6 %shard_map.60 = (f32[64,512]{1,0:T(8,128)}, f32[64,128]{1,0:T(8,128)}) custom-call(f32[64,512]{1,0:T(8,128)} %get-tuple-element.6.res_in, f32[64,128]{1,0:T(8,128)} %get-tuple-element.7.new_in), custom_call_target="tpu_custom_call" | custom-call | tf_op jit(solution)/shard_map/pallas_call | solution.py:508

commit v2 on v1

--- a/solution.py
+++ b/solution.py
@@ -22,6 +22,8 @@
 PLACE = {pair: at for at, pair in enumerate(PAIRS)}
 FIRST_ROWS = ((1, 0), (3, 0), (0, 1))
 LATER_ROWS = ((1, 1), (3, 1))
+SUM_TOP = 40
+TOP = 48
 
 
 def halves(x):
@@ -45,13 +47,13 @@
     c3, ccol, crow, s3, scol, r3, rrow, cof2,
     kh, kl, th, tl,
     pacc, pred, pred_in, res,
-    gpart, g_y, gsum, g_z, gall,
+    gpart, g_y, gsum, g_z, h_z, hsum, h_y, gall,
     upart, u_core, usum, u_in, uall,
     vpart, v_core, vsum, v_in,
     lhs_r, lhs_u,
     loc_sem, smp_send, smp_recv, row_send, row_recv, fwd_send, fwd_recv, rel_send, rel_recv,
     p_send, p_recv, q_send, q_recv,
-    gy_send, gy_recv, gz_send, gz_recv, az_send, az_recv, ay_send, ay_recv,
+    gy_send, gy_recv, gz_send, gz_recv, hz_send, hz_recv, hy_send, hy_recv, az_send, az_recv, ay_send, ay_recv,
     uc_send, uc_recv, ur_send, ur_recv, bz_send, bz_recv, by_send, by_recv,
     vc_send, vc_recv, vr_send, vr_recv,
 ):
@@ -86,15 +88,11 @@
     own_rows = pl.ds(pl.multiple_of(d * n, n), n)
     sib_rows = pl.ds(pl.multiple_of(sib * n, n), n)
     smp_load = load(samples, smp.at[0], loc_sem.at[0])
-    cen_loads = []
+    cen_loads, cof_loads = [], []
     for b in range(16):
         owner = ((y + b // 4) % 4 * 4 + (zh + b % 4) % 4) * 2 + core
         at = pl.ds(pl.multiple_of(owner * n, n), n)
         cen_loads.append(load(centres.at[at], cen.at[pl.ds(b * n, n)], loc_sem.at[5 + b]))
-    cof_loads = []
-    for b in range(16):
-        owner = ((y + b // 4) % 4 * 4 + (zh + b % 4) % 4) * 2 + core
-        at = pl.ds(pl.multiple_of(owner * n, n), n)
         cof_loads.append(load(coefs.at[:, at], cof.at[:, pl.ds(b * n, n)], loc_sem.at[21 + b]))
     tgt_load = load(targets, tgt, loc_sem.at[1])
     row_loads = [
@@ -108,18 +106,8 @@
         partners += [(d, centre_of(dx, dz)), (sib, centre_of(dx, dz))]
     for to in partners:
         pl.semaphore_signal(barrier, inc=1, device_id=to, device_id_type=MESH)
-    pl.semaphore_wait(barrier, len(partners))
 
     sends = []
-    smp_load.wait()
-    smp_copies = []
-    for i in range(4):
-        at = pl.ds(i * n, n)
-        copy = remote(smp.at[0, at], smp.at[1, at], smp_send.at[i], smp_recv.at[i], (sib, c))
-        copy.start()
-        smp_copies.append(copy)
-    sends += smp_copies
-    cen_loads[0].wait()
 
     def send_rows(pairs):
         for dx, dz in pairs:
@@ -157,11 +145,18 @@
     def await_forward(j):
         remote(rows.at[j, 0], rows.at[j, 1], fwd_send.at[j], fwd_recv.at[j], (sib, c)).wait_recv()
 
-    send_rows(FIRST_ROWS)
-
-    def norm_of(v):
-        total = jnp.sum(v * v, axis=1, keepdims=True) * SCALE_SQ
-        return jnp.broadcast_to(total, (n, n))
+    def norms_of(v, down, across):
+        hi, lo = halves(v * v * SCALE_SQ)
+        out = []
+        if down:
+            ones = jnp.ones((512, n), bf16)
+            out.append(jnp.dot(hi, ones, preferred_element_type=f32) + jnp.dot(lo, ones, preferred_element_type=f32))
+        if across:
+            ones = jnp.ones((16, 512), bf16)
+            a = lax.dot_general(ones, hi, NT, preferred_element_type=f32)
+            b = lax.dot_general(ones, lo, NT, preferred_element_type=f32)
+            out.append((a + b)[0:8, :])
+        return out
 
     def prepare_samples(half):
         def one(i, _):
@@ -172,7 +167,7 @@
             s3[to, 0:512] = hi
             s3[to, 512:1024] = hi
             s3[to, 1024:1536] = lo
-            scol[to, :] = norm_of(v) + EPS
+            scol[to, :] = norms_of(v, True, False)[0] + EPS
             return 0
 
         lax.fori_loop(0, 4, one, 0)
@@ -184,25 +179,38 @@
         c3[at, 0:512] = hi
         c3[at, 512:1024] = lo
         c3[at, 1024:1536] = hi
-        norms = norm_of(v)
-        ccol[at, :] = norms + EPS
-        crow[:, at] = norms.T[0:8, :]
+        down, across = norms_of(v, True, True)
+        ccol[at, :] = down + EPS
+        crow[:, at] = across
         w = cof[:, at]
         whi = w.astype(bf16).astype(f32)
         cof2[at, :] = jnp.concatenate([whi, w - whi], axis=0).T.astype(bf16)
         return 0
 
+    smp_load.wait()
     prepare_samples(0)
-    for copy in cen_loads[1:] + cof_loads:
-        copy.wait()
-    lax.fori_loop(0, 16, prepare_centres, 0)
-
-    tn = 512
+    for group in range(4):
+        for b in range(group * 4, group * 4 + 4):
+            cen_loads[b].wait()
+            cof_loads[b].wait()
+        lax.fori_loop(group * 4, group * 4 + 4, prepare_centres, 0)
+        if group == 0:
+            pl.semaphore_wait(barrier, len(partners))
+            smp_copies = []
+            for i in range(4):
+                at = pl.ds(i * n, n)
+                copy = remote(smp.at[0, at], smp.at[1, at], smp_send.at[i], smp_recv.at[i], (sib, c))
+                copy.start()
+                smp_copies.append(copy)
+            sends += smp_copies
+            send_rows(FIRST_ROWS)
+
+    tn = 1024
     pacc[...] = jnp.zeros_like(pacc)
 
     def data_tile(i, _):
-        mine = pl.ds(pl.multiple_of(i // 4 * 512, 512), 512)
-        at = pl.ds(pl.multiple_of(i % 4 * tn, tn), tn)
+        mine = pl.ds(pl.multiple_of(i // 2 * 512, 512), 512)
+        at = pl.ds(pl.multiple_of(i % 2 * tn, tn), tn)
         cross = lax.dot_general(s3[mine, :], c3[at, :], NT, preferred_element_type=f32)
         value = kernel_of(cross + lanes(scol[mine, :], tn // n) + crow[0:1, at])
         hi, lo = halves(value)
@@ -212,17 +220,17 @@
         pacc[mine, :] += jnp.dot(hi, w, preferred_element_type=f32) + jnp.dot(lo, w, preferred_element_type=f32)
         return 0
 
-    lax.fori_loop(0, 4, data_tile, 0)
+    lax.fori_loop(0, 2, data_tile, 0)
     for copy in smp_copies:
         copy.wait_recv()
     prepare_samples(1)
-    lax.fori_loop(4, 6, data_tile, 0)
+    lax.fori_loop(2, 3, data_tile, 0)
     for pair in FIRST_ROWS:
         await_rows(PLACE[pair])
     relay_rows(0)
     for pair in FIRST_ROWS[::-1]:
         forward_rows(PLACE[pair])
-    lax.fori_loop(6, 8, data_tile, 0)
+    lax.fori_loop(3, 4, data_tile, 0)
     both = pacc[...].T
     pred[...] = both[0:64] + both[64:128]
 
@@ -242,7 +250,7 @@
     for copy in row_loads:
         copy.wait()
 
-    tm = 512
+    tm = 1024
 
     def square(j, _):
         for kk in (0, 1):
@@ -252,7 +260,7 @@
             r3[to, 0:512] = hi
             r3[to, 512:1024] = hi
             r3[to, 1024:1536] = lo
-            rrow[:, to] = norm_of(v).T[0:8, :]
+            rrow[:, to] = norms_of(v, False, True)[0]
         cols = pl.ds(pl.multiple_of(j * 256, 256), 256)
 
         def tile(i, _):
@@ -297,23 +305,32 @@
         lhs_r[0:64, kk * 512 : kk * 512 + 512] = lo
         lhs_r[64:128, kk * 512 : kk * 512 + 512] = hi
     gy_copies = []
+    top = pl.ds(0, SUM_TOP)
+    low = pl.ds(SUM_TOP, 64 - SUM_TOP)
     for dy in (2, 1, 3, 0):
         at = slice(dy * 512, dy * 512 + 512)
         a = jnp.dot(lhs_r[...], kh[:, at], preferred_element_type=f32)
         b = jnp.dot(lhs_r[64:128, :], kl[:, at], preferred_element_type=f32)
         gpart[dy] = a[0:64] + a[64:128] + b
         if dy:
-            copy = remote(gpart.at[dy], g_y.at[dy - 1], gy_send.at[dy - 1], gy_recv.at[dy - 1], at_y(dy))
+            copy = remote(gpart.at[dy, top], g_y.at[dy - 1], gy_send.at[dy - 1], gy_recv.at[dy - 1], at_y(dy))
             copy.start()
             gy_copies.append(copy)
-    sends += gy_copies
+    hz_copies = []
+    for dz in (2, 1, 3):
+        copy = remote(
+            gpart.at[:, low, pl.ds(dz * n, n)], h_z.at[dz - 1], hz_send.at[dz - 1], hz_recv.at[dz - 1], at_z(dz)
+        )
+        copy.start()
+        hz_copies.append(copy)
+    sends += gy_copies + hz_copies
     res_out[...] = res[0]
     await_forward(3)
     await_forward(4)
     lax.fori_loop(3, 5, square, 0)
     for copy in gy_copies:
         copy.wait_recv()
-    gsum[...] = gpart[0] + g_y[0] + g_y[1] + g_y[2]
+    gsum[...] = gpart[0, 0:SUM_TOP] + g_y[0] + g_y[1] + g_y[2]
     gz_copies = []
     for dz in (2, 1, 3):
         copy = remote(
@@ -321,53 +338,88 @@
         )
         copy.start()
         gz_copies.append(copy)
-    sends += gz_copies
+    for copy in hz_copies:
+        copy.wait_recv()
+    hsum[...] = gpart[:, SUM_TOP:64, 0:n] + h_z[0] + h_z[1] + h_z[2]
+    hy_copies = []
+    for dy in (2, 1, 3):
+        copy = remote(hsum.at[dy], h_y.at[dy - 1], hy_send.at[dy - 1], hy_recv.at[dy - 1], at_y(dy))
+        copy.start()
+        hy_copies.append(copy)
+    sends += gz_copies + hy_copies
     for pair in LATER_ROWS:
         await_rows(PLACE[pair])
     relay_rows(1)
     for pair in LATER_ROWS:
         forward_rows(PLACE[pair])
-    for copy in gz_copies:
-        copy.wait_recv()
-    gall[0, :, 0:n] = gsum[:, 0:n] + g_z[0] + g_z[1] + g_z[2]
-
-    def spread_z(buf, send, recv):
+    for copy in gz_copies + hy_copies:
+        copy.wait_recv()
+    gall[0, 0:SUM_TOP, 0:n] = gsum[:, 0:n] + g_z[0] + g_z[1] + g_z[2]
+    gall[0, SUM_TOP:64, 0:n] = hsum[0] + h_y[0] + h_y[1] + h_y[2]
+
+    def spread_first(buf, send, recv):
+        rest = buf.shape[1] - TOP
+        along_z, along_y = [], []
+        for j in (2, 1, 3):
+            to = (4 - j) % 4
+            copy = remote(
+                buf.at[0, pl.ds(0, TOP), pl.ds(0, n)], buf.at[0, pl.ds(0, TOP), pl.ds(to * n, n)],
+                send.at[j - 1], recv.at[j - 1], at_z(j),
+            )
+            copy.start()
+            along_z.append(copy)
+            part = pl.ds(TOP, rest), pl.ds(0, n)
+            copy = remote(buf.at[(0, *part)], buf.at[(to, *part)], send.at[j + 2], recv.at[j + 2], at_y(j))
+            copy.start()
+            along_y.append(copy)
+        sends.extend(along_z + along_y)
+        return along_z, along_y
+
+    def spread_rest(buf, send, recv, along_y):
+        rest = buf.shape[1] - TOP
+        for copy in along_y:
+            copy.wait_recv()
         copies = []
-        for dz in (2, 1, 3):
-            to = (4 - dz) % 4
+        for j in (2, 1, 3):
+            to = (4 - j) % 4
             copy = remote(
-                buf.at[0, :, pl.ds(0, n)], buf.at[0, :, pl.ds(to * n, n)], send.at[dz - 1], recv.at[dz - 1], at_z(dz)
+                buf.at[:, pl.ds(TOP, rest), pl.ds(0, n)], buf.at[:, pl.ds(TOP, rest), pl.ds(to * n, n)],
+                send.at[j - 1], recv.at[j - 1], at_z(j),
             )
             copy.start()
             copies.append(copy)
         sends.extend(copies)
         return copies
 
-    def spread_y(buf, send, recv):
-        copies = []
-        for dy in (2, 1, 3):
-            copy = remote(buf.at[0], buf.at[(4 - dy) % 4], send.at[dy - 1], recv.at[dy - 1], at_y(dy))
-            copy.start()
-            copies.append(copy)
-        sends.extend(copies)
+    def spread_top(buf, send, recv, along_z):
+        for copy in along_z:
+            copy.wait_recv()
+        copies = {}
+        for j in (2, 1, 3):
+            to = (4 - j) % 4
+            part = buf.at[0, pl.ds(0, TOP)]
+            copy = remote(part, buf.at[to, pl.ds(0, TOP)], send.at[j + 2], recv.at[j + 2], at_y(j))
+            copy.start()
+            copies[to] = copy
+        sends.extend(copies.values())
         return copies
 
-    az_copies = spread_z(gall, az_send, az_recv)
+    along_z, along_y = spread_first(gall, az_send, az_recv)
     await_forward(5)
-    await_forward(6)
-    lax.fori_loop(5, 7, square, 0)
-    for copy in az_copies:
-        copy.wait_recv()
+    lax.fori_loop(5, 6, square, 0)
+    rest = spread_rest(gall, ay_send, ay_recv, along_y)
+    tops = spread_top(gall, ay_send, ay_recv, along_z)
     await_relayed(1)
     forward_rows(7)
-    ay_copies = spread_y(gall, ay_send, ay_recv)
+    await_forward(6)
+    lax.fori_loop(6, 7, square, 0)
     await_forward(7)
     lax.fori_loop(7, 8, square, 0)
-    def project(buf, out, arrivals, ones, finish):
+    def project(buf, out, rest, tops, ones, finish):
         top = 144 if ones else 128
         for dy in (0, 1, 3, 2):
-            if dy:
-                arrivals[(4 - dy) % 4].wait_recv()
+            for copy in [tops[dy]] if dy else rest:
+                copy.wait_recv()
             hi, lo = halves(buf[dy, 0:64, :])
             lhs_u[0:64, :] = lo
             lhs_u[64:128, :] = hi
@@ -413,7 +465,7 @@
     def finish_u(j):
         swaps[j] = swap_core(upart, u_core, uc_send, uc_recv, j)
 
-    project(gall, upart, {i: copy for i, copy in zip((2, 1, 3), ay_copies)}, True, finish_u)
+    project(gall, upart, rest, tops, True, finish_u)
     owners = []
     for j in (7, 6, 5, 4, 3, 2, 1, 0):
         swaps[j].wait_recv()
@@ -428,28 +480,28 @@
     uall[0, 0:64, 0:n] = total[0:64]
     uall[0, 64:72, 0:n] = jnp.broadcast_to(jnp.max(total[64:72], axis=1, keepdims=True), (8, n))
 
-    for copy in spread_z(uall, bz_send, bz_recv):
-        copy.wait_recv()
-    by_copies = spread_y(uall, by_send, by_recv)
-
-    tops = []
+    along_z, along_y = spread_first(uall, bz_send, bz_recv)
+    rest = spread_rest(uall, by_send, by_recv, along_y)
+    tops = spread_top(uall, by_send, by_recv, along_z)
+
+    found = []
 
     def finish_v(j):
-        if not tops:
+        if not found:
             largest = uall[0, 64:72, 0:n]
             for dy in range(4):
                 for dz in range(4):
                     largest = jnp.maximum(largest, uall[dy, 64:72, dz * n : dz * n + n])
-            tops.append(largest)
-        vpart[64:72, (2 * j + 1) * n : (2 * j + 2) * n] = tops[0]
+            found.append(largest)
+        vpart[64:72, (2 * j + 1) * n : (2 * j + 2) * n] = found[0]
         swaps[j] = swap_core(vpart, v_core, vc_send, vc_recv, j)
 
-    project(uall, vpart, {i: copy for i, copy in zip((2, 1, 3), by_copies)}, False, finish_v)
+    project(uall, vpart, rest, tops, False, finish_v)
     owners = []
     for j in (7, 6, 5, 4, 3, 2, 1, 0):
         swaps[j].wait_recv()
         vsum[j, 0:64] = vpart[0:64, 2 * j * n : 2 * j * n + n] + v_core[j, 0:64]
-        vsum[j, 64:72] = jnp.maximum(tops[0], v_core[j, 64:72])
+        vsum[j, 64:72] = jnp.maximum(found[0], v_core[j, 64:72])
         if j:
             owners.append(to_owner(vsum, v_in, vr_send, vr_recv, j))
     for copy in owners:
@@ -489,7 +541,8 @@
             vmem((2048, 128), bf16),
             vmem((1024, 2048), bf16), vmem((1024, 2048), bf16), vmem((2048, 2048), bf16), vmem((2048, 2048), bf16),
             vmem((1024, 128), f32), vmem((64, 1024), f32), vmem((15, 8, 512), f32), vmem((2, 64, 512), f32),
-            vmem((4, 64, 512), f32), vmem((3, 64, 512), f32), vmem((64, 512), f32), vmem((3, 64, 128), f32),
+            vmem((4, 64, 512), f32), vmem((3, SUM_TOP, 512), f32), vmem((SUM_TOP, 512), f32), vmem((3, SUM_TOP, 128), f32),
+            vmem((3, 4, 64 - SUM_TOP, 128), f32), vmem((4, 64 - SUM_TOP, 128), f32), vmem((3, 64 - SUM_TOP, 128), f32),
             vmem((4, 64, 512), f32),
             vmem((72, 2048), f32), vmem((8, 72, 128), f32), vmem((8, 72, 128), f32), vmem((7, 72, 128), f32),
             vmem((4, 72, 512), f32),
@@ -498,7 +551,8 @@
             dma((37,)), dma((4,)), dma((4,)), dma((8,)), dma((8,)), dma((8,)), dma((8,)), dma((4,)), dma((4,)),
             dma((15,)), dma((15,)), dma((15,)), dma((15,)),
             dma((3,)), dma((3,)), dma((3,)), dma((3,)), dma((3,)), dma((3,)), dma((3,)), dma((3,)),
-            dma((8,)), dma((8,)), dma((7,)), dma((7,)), dma((3,)), dma((3,)), dma((3,)), dma((3,)),
+            dma((6,)), dma((6,)), dma((6,)), dma((6,)),
+            dma((8,)), dma((8,)), dma((7,)), dma((7,)), dma((6,)), dma((6,)), dma((6,)), dma((6,)),
             dma((8,)), dma((8,)), dma((7,)), dma((7,)),
         ],
         compiler_params=pltpu.CompilerParams(

time: 107 us -> 110 us (1.028)
  Pallas kernels: 107 us -> 109 us
    pallas_call x1, Pallas kernels: 105 us -> 107 us  [body(): pl.pallas_call(step_kernel, out_shape=(jax.ShapeDtypeStruct((64, 512), f3...]
where the time goes in v2:
time: 110 us
  Pallas kernels  109 us (99%)
    pallas_call x1, Pallas kernels, body(): pl.pallas_call(step_kernel, out_shape=(jax.ShapeDtypeStruct((64, 512), f3...  107 us

profile of v2, /device:TPU:1, one launch (start us, length us, event | category | flops | bytes accessed | tf_op | source)
XLA Modules:
  0.0 109.6 jit_solution(6734674900003786873)
XLA Ops:
  0.6 107.4 %shard_map.59 = (f32[64,512]{1,0:T(8,128)}, f32[64,128]{1,0:T(8,128)}) custom-call(f32[512,512]{1,0:T(8,128)} %samples.1, f32[64,512]{1,0:T(8,128)} %bitcast.5, f32[4096,512]{1,0:T(8,128)} %centres.1, f32[64,4096]{1,0:T(8,128)} %bitcast.4), custom_call_target="tpu_custom_call" | custom-call | tf_op jit(solution)/shard_map/pallas_call | solution.py:531
  108.1 1.6 %shard_map.60 = (f32[64,512]{1,0:T(8,128)}, f32[64,128]{1,0:T(8,128)}) custom-call(f32[64,512]{1,0:T(8,128)} %get-tuple-element.6.res_in, f32[64,128]{1,0:T(8,128)} %get-tuple-element.7.new_in), custom_call_target="tpu_custom_call" | custom-call | tf_op jit(solution)/shard_map/pallas_call | solution.py:562
